TPU v7x, 256 devices: a whole 4x4x8 slice. The times are simulated.
256 devices in a mesh: src: 16 (over z, y_hi), tgt: 16 (over x, y_lo, core).
Axes of the slice: x: 4, y: 4 (y_hi: 2, y_lo: 2; y = y_hi * 2 + y_lo), z: 8, core: 2. Of those that a mesh axis runs over, the one named last changes fastest.
Arguments:
- frame_one: bfloat16 [256, 256, 128], P(('src', 'tgt')), may hold values from -36 to 36
- frame_two: bfloat16 [256, 256, 128], P(('src', 'tgt')), may hold values from -36 to 36
- conv_weight: bfloat16 [9, 128, 128], replicated, may hold values from -0.1875 to 0.1875
- proj_weight: bfloat16 [128, 128], replicated, may hold values from -0.5 to 0.5
Outputs:
- flow_forward: float32 [2, 256, 256], P(None, ('src', 'tgt'))
- flow_backward: float32 [2, 256, 256], P(None, ('src', 'tgt'))
All inputs are finite; a program needn't handle non-finite values.
Results may differ from a plain program's by a relative error of at most 0.012.
The roundings to bfloat16 on the way count: a program that leaves them out, or rounds other values in their place, can miss the bound.
Values may be sent and summed in bfloat16 or wider, within the bound.
A program may use at most 64 MiB of HBM per device.

v0:
```python
import math
import jax
import jax.numpy as jnp
from jax import lax
from jax.sharding import PartitionSpec as P


def padded_2(block, sides, width):
    for axis, dim in sides:
        count = lax.axis_size(axis)
        forward = [(i, i + 1) for i in range(count - 1)]
        backward = [(target, source) for source, target in forward]
        low = lax.ppermute(
            lax.slice_in_dim(block, block.shape[dim] - width, None, axis=dim), axis, forward
        )
        high = lax.ppermute(lax.slice_in_dim(block, 0, width, axis=dim), axis, backward)
        block = jnp.concatenate([low, block, high], axis=dim)
    return block


def merged(value, axis, join):
    pieces = jax.tree.map(lambda part: lax.all_gather(part, axis), value)
    head = jax.tree.map(lambda part: part[0], pieces)
    tail = jax.tree.map(lambda part: part[1:], pieces)
    subtotal, _ = lax.scan(lambda subtotal, piece: (join(subtotal, piece), None), head, tail)
    return subtotal


def encode(stacked, conv_weight, proj_weight):
    padded = padded_2(stacked, ((("src", "tgt"), 1),), 1)
    padded = jnp.pad(padded, ((0, 0), (0, 0), (1, 1), (0, 0)))
    strip_rows, columns = (stacked.shape[1], stacked.shape[2])
    total = jnp.zeros(stacked.shape, jnp.float32)
    for offset_row in range(3):
        for offset_col in range(3):
            window = padded[
                :, offset_row : offset_row + strip_rows, offset_col : offset_col + columns, :
            ]
            total = total + jnp.dot(
                window, conv_weight[3 * offset_row + offset_col], preferred_element_type=jnp.float32
            )
    hidden = jax.nn.relu(total).astype(jnp.bfloat16)
    mixed = stacked.astype(jnp.float32) + jnp.dot(
        hidden, proj_weight, preferred_element_type=jnp.float32
    )
    return mixed.astype(jnp.bfloat16)


def merge_pair(former, latter):
    highest = jnp.maximum(former[0], latter[0])
    keep_former = jnp.exp(former[0] - highest)
    keep_latter = jnp.exp(latter[0] - highest)
    return (
        highest,
        former[1] * keep_former + latter[1] * keep_latter,
        former[2] * keep_former + latter[2] * keep_latter,
        former[3] * keep_former + latter[3] * keep_latter,
    )


def tile_stats(piece_block, block_x, block_y, fixed_flat, fixed_x, fixed_y, factor):
    scores = (
        lax.dot_general(
            piece_block, fixed_flat, (((1,), (1,)), ((), ())), preferred_element_type=jnp.float32
        )
        * factor
    )
    row_top = jnp.max(scores, axis=1)
    row_weights = jnp.exp(scores - row_top[:, None])
    row_stats = (
        row_top,
        jnp.sum(row_weights, axis=1),
        jnp.sum(row_weights * fixed_x[None, :], axis=1),
        jnp.sum(row_weights * fixed_y[None, :], axis=1),
    )
    column_top = jnp.max(scores, axis=0)
    column_weights = jnp.exp(scores - column_top[None, :])
    column_stats = (
        column_top,
        jnp.sum(column_weights, axis=0),
        jnp.sum(column_weights * block_x[:, None], axis=0),
        jnp.sum(column_weights * block_y[:, None], axis=0),
    )
    return (row_stats, column_stats)


def on_device(frame_one, frame_two, conv_weight, proj_weight):
    features = encode(jnp.stack([frame_one, frame_two]), conv_weight, proj_weight)
    source_feat = features[0]
    target_feat = features[1]
    strip_rows, columns, channels = frame_one.shape
    src_index = lax.axis_index("src")
    tgt_index = lax.axis_index("tgt")
    src_count = lax.axis_size("src")
    tgt_count = lax.axis_size("tgt")
    factor = 1.0 / math.sqrt(channels)
    source_pixels = strip_rows * tgt_count * columns
    target_pixels = strip_rows * src_count * columns
    own_pixels = strip_rows * columns

    def pixel_coords(row_numbers):
        coord_y = jnp.repeat(row_numbers.astype(jnp.float32), columns)
        coord_x = jnp.tile(jnp.arange(columns, dtype=jnp.float32), row_numbers.shape[0])
        return (coord_x, coord_y)

    def empty_stats(count):
        zeros_line = jnp.zeros((count,), jnp.float32)
        return (jnp.full((count,), -jnp.inf, jnp.float32), zeros_line, zeros_line, zeros_line)

    target_tile = lax.all_gather(target_feat, "src", axis=0, tiled=True)
    whole_row = jnp.arange(strip_rows * src_count, dtype=jnp.int32)
    tile_x, tile_y = pixel_coords(
        (whole_row // strip_rows * tgt_count + tgt_index) * strip_rows + whole_row % strip_rows
    )
    fixed_flat = target_tile.reshape(-1, channels)
    shard_piece = lax.all_gather(source_feat, "tgt", axis=0, tiled=True)
    piece_rows = shard_piece.shape[0]
    block_rows = math.gcd(piece_rows, max(1, 512 // columns))
    blocks = piece_rows // block_rows
    block_size = block_rows * columns
    piece_x, piece_y = pixel_coords(
        src_index * tgt_count * strip_rows + jnp.arange(piece_rows, dtype=jnp.int32)
    )

    def block_step(fixed_acc, block_item):
        piece_block, block_x, block_y = block_item
        row_stats, column_stats = tile_stats(
            piece_block, block_x, block_y, fixed_flat, tile_x, tile_y, factor
        )
        return (merge_pair(fixed_acc, column_stats), row_stats)

    fixed_acc, row_parts = lax.scan(
        block_step,
        (empty_stats(target_pixels), empty_stats(source_pixels))[0],
        (
            shard_piece.reshape(blocks, block_size, channels),
            piece_x.reshape(blocks, block_size),
            piece_y.reshape(blocks, block_size),
        ),
    )
    placed = tuple((segment.reshape(-1) for segment in row_parts))
    fixed_acc, piece_acc = (fixed_acc, placed)
    source_stats, target_stats = (piece_acc, fixed_acc)
    own_x, own_y = pixel_coords(
        (src_index * tgt_count + tgt_index) * strip_rows + jnp.arange(strip_rows, dtype=jnp.int32)
    )
    merged_rows = merged(source_stats, "tgt", merge_pair)
    merged_cols = merged(target_stats, "src", merge_pair)
    source_sums = [
        lax.dynamic_slice_in_dim(member, tgt_index * own_pixels, own_pixels, 0)
        for member in merged_rows[1:]
    ]
    target_sums = [
        lax.dynamic_slice_in_dim(member, src_index * own_pixels, own_pixels, 0)
        for member in merged_cols[1:]
    ]
    flow_forward = jnp.stack(
        [source_sums[1] / source_sums[0] - own_x, source_sums[2] / source_sums[0] - own_y]
    ).reshape(2, strip_rows, columns)
    flow_backward = jnp.stack(
        [target_sums[1] / target_sums[0] - own_x, target_sums[2] / target_sums[0] - own_y]
    ).reshape(2, strip_rows, columns)
    return (flow_forward, flow_backward)


def solution(mesh):
    in_specs = (P(("src", "tgt"), None, None), P(("src", "tgt"), None, None), P(), P())
    out_specs = (P(None, ("src", "tgt"), None), P(None, ("src", "tgt"), None))
    return jax.shard_map(
        on_device, mesh=mesh, in_specs=in_specs, out_specs=out_specs, check_vma=False
    )
```

profile of v0, /device:TPU:16, one launch (start us, length us, event | category | flops | bytes accessed | tf_op | source)
XLA Modules:
  0.0 487.1 jit_solution(11007126470495487609)
XLA Ops:
  8.1 1.9 collective-permute-start
  10.0 5.8 %collective-permute-start.1 = (bf16[2,1,256,128]{3,2,1,0:T(8,128)(2,1)S(1)}, bf16[2,1,256,128]{3,2,1,0:T(8,128)(2,1)S(1)}, u32[]{:S(2)}, u32[]{:S(2)}) collective-permute-start(bf16[2,1,256,128]{3,2,1,0:T(8,128)(2,1)S(1)} %pad_maximum_fusion), channel_id=1, source_target_pairs={{1,0},{2,1},{3,2},{4,3},{5,4},{6,5},{7,6},{8,7},{9,8},{10,9},{11,1... | collective-permute-start | bytes 393224 | tf_op jit(solution)/shard_map/ppermute | solution.py:16
  16.5 1.8 collective-permute-done.1
  29.7 39.2 %all-gather.11.cloned.1.call-done = bf16[16,256,128]{2,1,0:T(8,128)(2,1)} async-done(((bf16[1,256,128]{2,1,0:T(8,128)(2,1)}), bf16[16,256,128]{2,1,0:T(8,128)(2,1)}) %all-gather.11.cloned.1.call-update) | async-done | bytes 1048592 | tf_op jit(solution)/shard_map/all_gather | solution.py:116
  69.0 79.3 %all-gather.13.cloned.1.call-done = bf16[16,256,128]{2,1,0:T(8,128)(2,1)} async-done(((bf16[1,256,128]{2,1,0:T(8,128)(2,1)}), bf16[16,256,128]{2,1,0:T(8,128)(2,1)}) %all-gather.13.cloned.1.call-update) | async-done | bytes 1048592 | tf_op jit(solution)/shard_map/all_gather | solution.py:110
  148.3 94.9 %while.59 = (s32[]{:T(128)}, f32[4096]{0:T(1024)S(1)}, f32[4096]{0:T(1024)S(1)}, f32[4096]{0:T(1024)S(1)}, f32[4096]{0:T(1024)S(1)}, /*index=5*/f32[8,512]{1,0:T...) while((s32[]{:T(128)}, f32[4096]{0:T(1024)S(1)}, ...), condition=%wide.region_9.10_spmd.clone, body=%wide.region_0.9_spmd.clone.sunk | while | flops 570484736 | bytes 18488048 | solution.py:132
  148.3 2.6 multiply_reduce_fusion.8
  151.1 8.7 %multiply_reduce_fusion.9 = (f32[512]{0:T(512)S(1)}, f32[512]{0:T(512)S(1)}, f32[512]{0:T(512)S(1)}, f32[4096]{0:T(1024)S(1)}, f32[4096]{0:T(1024)S(1)}, /*index=5*/f32[4096]{0:T(1024)S(1)}) fusion(f32[512,4096]{1,0:T(8,128)S(1)} %get-tuple-element.596, f32[4096]{0:T(1024)S(1)} %bitcast.168, f32[512]{0:T(512)S(1)} %get-tuple-element.597, ...), kind=kLoop, calls=%fused_computation.20.clone.1 | loop fusion | flops 27249152 | bytes 8499200 | tf_op jit(solution)/shard_map/while/body/eval_jaxpr/reduce_sum | solution.py:74
  160.2 2.6 multiply_reduce_fusion.8
  162.9 8.7 %multiply_reduce_fusion.9 = (f32[512]{0:T(512)S(1)}, f32[512]{0:T(512)S(1)}, f32[512]{0:T(512)S(1)}, f32[4096]{0:T(1024)S(1)}, f32[4096]{0:T(1024)S(1)}, /*index=5*/f32[4096]{0:T(1024)S(1)}) fusion(f32[512,4096]{1,0:T(8,128)S(1)} %get-tuple-element.596, f32[4096]{0:T(1024)S(1)} %bitcast.168, f32[512]{0:T(512)S(1)} %get-tuple-element.597, ...), kind=kLoop, calls=%fused_computation.20.clone.1 | loop fusion | flops 27249152 | bytes 8499200 | tf_op jit(solution)/shard_map/while/body/eval_jaxpr/reduce_sum | solution.py:74
  172.0 2.6 multiply_reduce_fusion.8
  174.8 8.7 %multiply_reduce_fusion.9 = (f32[512]{0:T(512)S(1)}, f32[512]{0:T(512)S(1)}, f32[512]{0:T(512)S(1)}, f32[4096]{0:T(1024)S(1)}, f32[4096]{0:T(1024)S(1)}, /*index=5*/f32[4096]{0:T(1024)S(1)}) fusion(f32[512,4096]{1,0:T(8,128)S(1)} %get-tuple-element.596, f32[4096]{0:T(1024)S(1)} %bitcast.168, f32[512]{0:T(512)S(1)} %get-tuple-element.597, ...), kind=kLoop, calls=%fused_computation.20.clone.1 | loop fusion | flops 27249152 | bytes 8499200 | tf_op jit(solution)/shard_map/while/body/eval_jaxpr/reduce_sum | solution.py:74
  183.9 2.6 multiply_reduce_fusion.8
  186.7 8.7 %multiply_reduce_fusion.9 = (f32[512]{0:T(512)S(1)}, f32[512]{0:T(512)S(1)}, f32[512]{0:T(512)S(1)}, f32[4096]{0:T(1024)S(1)}, f32[4096]{0:T(1024)S(1)}, /*index=5*/f32[4096]{0:T(1024)S(1)}) fusion(f32[512,4096]{1,0:T(8,128)S(1)} %get-tuple-element.596, f32[4096]{0:T(1024)S(1)} %bitcast.168, f32[512]{0:T(512)S(1)} %get-tuple-element.597, ...), kind=kLoop, calls=%fused_computation.20.clone.1 | loop fusion | flops 27249152 | bytes 8499200 | tf_op jit(solution)/shard_map/while/body/eval_jaxpr/reduce_sum | solution.py:74
  195.7 2.6 multiply_reduce_fusion.8
  198.5 8.7 %multiply_reduce_fusion.9 = (f32[512]{0:T(512)S(1)}, f32[512]{0:T(512)S(1)}, f32[512]{0:T(512)S(1)}, f32[4096]{0:T(1024)S(1)}, f32[4096]{0:T(1024)S(1)}, /*index=5*/f32[4096]{0:T(1024)S(1)}) fusion(f32[512,4096]{1,0:T(8,128)S(1)} %get-tuple-element.596, f32[4096]{0:T(1024)S(1)} %bitcast.168, f32[512]{0:T(512)S(1)} %get-tuple-element.597, ...), kind=kLoop, calls=%fused_computation.20.clone.1 | loop fusion | flops 27249152 | bytes 8499200 | tf_op jit(solution)/shard_map/while/body/eval_jaxpr/reduce_sum | solution.py:74
  207.6 2.6 multiply_reduce_fusion.8
  210.4 8.7 %multiply_reduce_fusion.9 = (f32[512]{0:T(512)S(1)}, f32[512]{0:T(512)S(1)}, f32[512]{0:T(512)S(1)}, f32[4096]{0:T(1024)S(1)}, f32[4096]{0:T(1024)S(1)}, /*index=5*/f32[4096]{0:T(1024)S(1)}) fusion(f32[512,4096]{1,0:T(8,128)S(1)} %get-tuple-element.596, f32[4096]{0:T(1024)S(1)} %bitcast.168, f32[512]{0:T(512)S(1)} %get-tuple-element.597, ...), kind=kLoop, calls=%fused_computation.20.clone.1 | loop fusion | flops 27249152 | bytes 8499200 | tf_op jit(solution)/shard_map/while/body/eval_jaxpr/reduce_sum | solution.py:74
  219.5 2.6 multiply_reduce_fusion.8
  222.3 8.7 %multiply_reduce_fusion.9 = (f32[512]{0:T(512)S(1)}, f32[512]{0:T(512)S(1)}, f32[512]{0:T(512)S(1)}, f32[4096]{0:T(1024)S(1)}, f32[4096]{0:T(1024)S(1)}, /*index=5*/f32[4096]{0:T(1024)S(1)}) fusion(f32[512,4096]{1,0:T(8,128)S(1)} %get-tuple-element.596, f32[4096]{0:T(1024)S(1)} %bitcast.168, f32[512]{0:T(512)S(1)} %get-tuple-element.597, ...), kind=kLoop, calls=%fused_computation.20.clone.1 | loop fusion | flops 27249152 | bytes 8499200 | tf_op jit(solution)/shard_map/while/body/eval_jaxpr/reduce_sum | solution.py:74
  231.3 2.6 multiply_reduce_fusion.8
  234.1 8.7 %multiply_reduce_fusion.9 = (f32[512]{0:T(512)S(1)}, f32[512]{0:T(512)S(1)}, f32[512]{0:T(512)S(1)}, f32[4096]{0:T(1024)S(1)}, f32[4096]{0:T(1024)S(1)}, /*index=5*/f32[4096]{0:T(1024)S(1)}) fusion(f32[512,4096]{1,0:T(8,128)S(1)} %get-tuple-element.596, f32[4096]{0:T(1024)S(1)} %bitcast.168, f32[512]{0:T(512)S(1)} %get-tuple-element.597, ...), kind=kLoop, calls=%fused_computation.20.clone.1 | loop fusion | flops 27249152 | bytes 8499200 | tf_op jit(solution)/shard_map/while/body/eval_jaxpr/reduce_sum | solution.py:74
  243.2 20.8 %all-gather.4 = f32[16,1,4096]{2,1,0:T(1,128)S(1)} all-gather(f32[1,1,4096]{2,1,0:T(1,128)S(1)} %reshape.124), channel_id=1, replica_groups=mesh['src'=16,'tgt'=16] {'tgt'}, dimensions={0}, use_global_device_ids=true | all-gather | bytes 278528 | tf_op jit(solution)/shard_map/all_gather | solution.py:22
  264.1 17.0 %all-gather.5 = f32[16,1,4096]{2,1,0:T(1,128)S(1)} all-gather(f32[1,1,4096]{2,1,0:T(1,128)S(1)} %reshape.126), channel_id=1, replica_groups=mesh['src'=16,'tgt'=16] {'tgt'}, dimensions={0}, use_global_device_ids=true | all-gather | bytes 278528 | tf_op jit(solution)/shard_map/all_gather | solution.py:22
  281.2 18.5 %all-gather.6 = f32[16,1,4096]{2,1,0:T(1,128)S(1)} all-gather(f32[1,1,4096]{2,1,0:T(1,128)S(1)} %reshape.128), channel_id=1, replica_groups=mesh['src'=16,'tgt'=16] {'tgt'}, dimensions={0}, use_global_device_ids=true | all-gather | bytes 278528 | tf_op jit(solution)/shard_map/all_gather | solution.py:22
  299.7 17.0 %all-gather.7 = f32[16,1,4096]{2,1,0:T(1,128)S(1)} all-gather(f32[1,1,4096]{2,1,0:T(1,128)S(1)} %reshape.130), channel_id=1, replica_groups=mesh['src'=16,'tgt'=16] {'tgt'}, dimensions={0}, use_global_device_ids=true | all-gather | bytes 278528 | tf_op jit(solution)/shard_map/all_gather | solution.py:22
  316.7 38.6 %all-gather = f32[65536]{0:T(1024)S(1)} all-gather(f32[4096]{0:T(1024)S(1)} %get-tuple-element.191), channel_id=2, replica_groups=mesh['src'=16,'tgt'=16] {'src'}, dimensions={0}, use_global_device_ids=true | all-gather | bytes 278528 | tf_op jit(solution)/shard_map/all_gather | solution.py:22
  355.3 40.5 %all-gather.1 = f32[65536]{0:T(1024)S(1)} all-gather(f32[4096]{0:T(1024)S(1)} %get-tuple-element.192), channel_id=3, replica_groups=mesh['src'=16,'tgt'=16] {'src'}, dimensions={0}, use_global_device_ids=true | all-gather | bytes 278528 | tf_op jit(solution)/shard_map/all_gather | solution.py:22
  395.9 37.1 %all-gather.2 = f32[65536]{0:T(1024)S(1)} all-gather(f32[4096]{0:T(1024)S(1)} %get-tuple-element.193), channel_id=4, replica_groups=mesh['src'=16,'tgt'=16] {'src'}, dimensions={0}, use_global_device_ids=true | all-gather | bytes 278528 | tf_op jit(solution)/shard_map/all_gather | solution.py:22
  433.0 40.5 %all-gather.3 = f32[65536]{0:T(1024)S(1)} all-gather(f32[4096]{0:T(1024)S(1)} %get-tuple-element.194), channel_id=5, replica_groups=mesh['src'=16,'tgt'=16] {'src'}, dimensions={0}, use_global_device_ids=true | all-gather | bytes 278528 | tf_op jit(solution)/shard_map/all_gather | solution.py:22
  474.1 2.4 while.57
  476.7 2.4 while.58
  (312 shorter events, 21.5 us)
Async XLA Ops:
  7.2 19.7 %copy-start = (bf16[128,128]{1,0:T(8,128)(2,1)S(1)}, bf16[128,128]{1,0:T(8,128)(2,1)}, u32[]{:S(2)}) copy-start(bf16[128,128]{1,0:T(8,128)(2,1)} %param.13) | copy-start | bytes 98308
  7.2 61.8 %all-gather.11.cloned.1.call-start = ((), (), s32[]{:S(2)}) async-start(), calls=%async_computation | async-start | bytes 1114112 | tf_op jit(solution)/shard_map/all_gather | solution.py:116
  8.1 8.4 %collective-permute-start = (bf16[2,1,256,128]{3,2,1,0:T(8,128)(2,1)S(1)}, bf16[2,1,256,128]{3,2,1,0:T(8,128)(2,1)S(1)}, u32[]{:S(2)}, u32[]{:S(2)}) collective-permute-start(bf16[2,1,256,128]{3,2,1,0:T(8,128)(2,1)S(1)} %pad_maximum_fusion), channel_id=1, source_target_pairs={{0,1},{1,2},{2,3},{3,4},{4,5},{5,6},{6,7},{7,8},{8,9},{9,10},{10,1... | collective-permute-start | bytes 393224 | tf_op jit(solution)/shard_map/ppermute | solution.py:13
  10.0 8.3 %collective-permute-start.1 = (bf16[2,1,256,128]{3,2,1,0:T(8,128)(2,1)S(1)}, bf16[2,1,256,128]{3,2,1,0:T(8,128)(2,1)S(1)}, u32[]{:S(2)}, u32[]{:S(2)}) collective-permute-start(bf16[2,1,256,128]{3,2,1,0:T(8,128)(2,1)S(1)} %pad_maximum_fusion), channel_id=1, source_target_pairs={{1,0},{2,1},{3,2},{4,3},{5,4},{6,5},{7,6},{8,7},{9,8},{10,9},{11,1... | collective-permute-start | bytes 393224 | tf_op jit(solution)/shard_map/ppermute | solution.py:16
  28.8 119.4 %all-gather.13.cloned.1.call-start = ((), (), s32[]{:S(2)}) async-start(), calls=%async_computation.1 | async-start | bytes 1114112 | tf_op jit(solution)/shard_map/all_gather | solution.py:110
Sparse Core Ops, SparseCore 0:
  28.9 39.9 all-gather.10
  71.5 76.6 all-gather.12
where the time goes:
time: 488 us; the launch traced here: 487 us
  blocking collectives  230 us (47%)
  waiting for transfers between devices  122 us (25%)
  other arithmetic  73.2 us (15%)
  matrix products  29.9 us (6%)
  between operations  14.4 us (3%)
  local copies, waits for them, and re-layouts  7.8 us (2%)
  starting transfers between devices  7.75 us (2%)
    all_gather x8, blocking collectives, merged(): pieces = jax.tree.map(lambda part: lax.all_gather(part, axis), value)  230 us
    all_gather x1, waiting for transfers between devices, on_device(): target_tile = lax.all_gather(target_feat, 'src', axis=0, tiled=True)  79.3 us
    reduce_sum x8, other arithmetic, tile_stats(): jnp.sum(row_weights * fixed_y[None, :], axis=1)  69.7 us
    all_gather x1, waiting for transfers between devices, on_device(): shard_piece = lax.all_gather(source_feat, 'tgt', axis=0, tiled=True)  39.2 us
    dot_general x8, matrix products, tile_stats(): lax.dot_general(piece_block, fixed_flat, (((1,), (1,)), ((), ())), prefer...  21.2 us
  transfers between devices with their start and end apart: 4, of which 4 were waited for; matrix products, arithmetic and copies ran while one was open for 0% of the time, Pallas kernels for 0%

commit v1 on v0

--- a/solution.py
+++ b/solution.py
@@ -113,7 +113,12 @@
         (whole_row // strip_rows * tgt_count + tgt_index) * strip_rows + whole_row % strip_rows
     )
     fixed_flat = target_tile.reshape(-1, channels)
-    shard_piece = lax.all_gather(source_feat, "tgt", axis=0, tiled=True)
+    shard_piece = jnp.concatenate(
+        lax.all_to_all(
+            jnp.stack([source_feat for _ in range(lax.axis_size("tgt"))], axis=0), "tgt", 0, 0
+        ),
+        axis=0,
+    )
     piece_rows = shard_piece.shape[0]
     block_rows = math.gcd(piece_rows, max(1, 512 // columns))
     blocks = piece_rows // block_rows

time: 488 us -> 453 us (0.928)
  waiting for transfers between devices: 122 us -> 77.4 us
  starting transfers between devices: 7.75 us -> 16 us
    all_gather x1 -> x0, waiting for transfers between devices: 39.2 us -> none  [on_device(): shard_piece = lax.all_gather(source_feat, 'tgt', axis=0, tiled=True)]
    all_gather x1, waiting for transfers between devices: 79.3 us -> 58.6 us  [on_device(): target_tile = lax.all_gather(target_feat, 'src', axis=0, tiled=True)]
    all_to_all x0 -> x1, waiting for transfers between devices: none -> 16.3 us  [on_device(): lax.all_to_all(jnp.stack([source_feat for _ in range(lax.axis_size('tgt')...]
    all_to_all x0 -> x1, starting transfers between devices: none -> 8.3 us  [on_device(): lax.all_to_all(jnp.stack([source_feat for _ in range(lax.axis_size('tgt')...]
where the time goes in v1:
time: 453 us; the launch traced here: 452 us
  blocking collectives  230 us (51%)
  waiting for transfers between devices  77.4 us (17%)
  other arithmetic  73.2 us (16%)
  matrix products  29.3 us (6%)
  starting transfers between devices  16 us (4%)
  between operations  14.4 us (3%)
  local copies, waits for them, and re-layouts  9 us (2%)
    all_gather x8, blocking collectives, merged(): pieces = jax.tree.map(lambda part: lax.all_gather(part, axis), value)  230 us
    reduce_sum x8, other arithmetic, tile_stats(): jnp.sum(row_weights * fixed_y[None, :], axis=1)  69.7 us
    all_gather x1, waiting for transfers between devices, on_device(): target_tile = lax.all_gather(target_feat, 'src', axis=0, tiled=True)  58.6 us
    dot_general x8, matrix products, tile_stats(): lax.dot_general(piece_block, fixed_flat, (((1,), (1,)), ((), ())), prefer...  20.6 us
    all_to_all x1, waiting for transfers between devices, on_device(): lax.all_to_all(jnp.stack([source_feat for _ in range(lax.axis_size('tgt')...  16.3 us
  transfers between devices with their start and end apart: 4, of which 4 were waited for; matrix products, arithmetic and copies ran while one was open for 0% of the time, Pallas kernels for 0%

profile of v1, /device:TPU:16, one launch (start us, length us, event | category | flops | bytes accessed | tf_op | source)
XLA Modules:
  0.0 451.6 jit_solution(11867758196710336091)
XLA Ops:
  8.1 1.9 collective-permute-start
  10.0 5.8 %collective-permute-start.1 = (bf16[2,1,256,128]{3,2,1,0:T(8,128)(2,1)S(1)}, bf16[2,1,256,128]{3,2,1,0:T(8,128)(2,1)S(1)}, u32[]{:S(2)}, u32[]{:S(2)}) collective-permute-start(bf16[2,1,256,128]{3,2,1,0:T(8,128)(2,1)S(1)} %pad_maximum_fusion), channel_id=1, source_target_pairs={{1,0},{2,1},{3,2},{4,3},{5,4},{6,5},{7,6},{8,7},{9,8},{10,9},{11,1... | collective-permute-start | bytes 393224 | tf_op jit(solution)/shard_map/ppermute | solution.py:16
  30.0 8.3 %all-to-all-start = ((bf16[16,1,256,128]{3,2,1,0:T(8,128)(2,1)}), bf16[16,1,256,128]{3,2,1,0:T(8,128)(2,1)S(1)}, u32[]{:S(2)}, u32[]{:S(2)}) async-start(bf16[16,1,256,128]{3,2,1,0:T(8,128)(2,1)} %stack.36), calls=%async_computation | async-start | bytes 2097152 | tf_op jit(solution)/shard_map/all_to_all | solution.py:117
  38.5 16.3 %all-to-all-done = bf16[16,1,256,128]{3,2,1,0:T(8,128)(2,1)S(1)} async-done(((bf16[16,1,256,128]{3,2,1,0:T(8,128)(2,1)}), bf16[16,1,256,128]{3,2,1,0:T(8,128)(2,1)S(1)}, u32[]{:S(2)}, u32[]{:S(2)}) %all-to-all-start) | async-done | bytes 1048608 | tf_op jit(solution)/shard_map/all_to_all | solution.py:117
  54.8 58.6 %all-gather.10.cloned.1.call-done = bf16[16,256,128]{2,1,0:T(8,128)(2,1)} async-done(((bf16[1,256,128]{2,1,0:T(8,128)(2,1)}), bf16[16,256,128]{2,1,0:T(8,128)(2,1)}) %all-gather.10.cloned.1.call-update) | async-done | bytes 1048592 | tf_op jit(solution)/shard_map/all_gather | solution.py:110
  113.4 94.3 %while.59 = (s32[]{:T(128)}, f32[4096]{0:T(1024)S(1)}, f32[4096]{0:T(1024)S(1)}, f32[4096]{0:T(1024)S(1)}, f32[4096]{0:T(1024)S(1)}, /*index=5*/f32[8,512]{1,0:T...) while((s32[]{:T(128)}, f32[4096]{0:T(1024)S(1)}, ...), condition=%wide.region_9.10_spmd.clone, body=%wide.region_0.9_spmd.clone.sunk | while | flops 570484736 | bytes 18487540 | solution.py:137
  113.4 2.6 multiply_reduce_fusion.8
  116.1 8.7 %multiply_reduce_fusion.9 = (f32[512]{0:T(512)S(1)}, f32[512]{0:T(512)S(1)}, f32[512]{0:T(512)S(1)}, f32[4096]{0:T(1024)S(1)}, f32[4096]{0:T(1024)S(1)}, /*index=5*/f32[4096]{0:T(1024)S(1)}) fusion(f32[512,4096]{1,0:T(8,128)S(1)} %get-tuple-element.596, f32[4096]{0:T(1024)S(1)} %bitcast.171, f32[512]{0:T(512)S(1)} %get-tuple-element.597, ...), kind=kLoop, calls=%fused_computation.20.clone.1 | loop fusion | flops 27249152 | bytes 8499200 | tf_op jit(solution)/shard_map/while/body/eval_jaxpr/reduce_sum | solution.py:74
  125.2 2.6 multiply_reduce_fusion.8
  127.9 8.7 %multiply_reduce_fusion.9 = (f32[512]{0:T(512)S(1)}, f32[512]{0:T(512)S(1)}, f32[512]{0:T(512)S(1)}, f32[4096]{0:T(1024)S(1)}, f32[4096]{0:T(1024)S(1)}, /*index=5*/f32[4096]{0:T(1024)S(1)}) fusion(f32[512,4096]{1,0:T(8,128)S(1)} %get-tuple-element.596, f32[4096]{0:T(1024)S(1)} %bitcast.171, f32[512]{0:T(512)S(1)} %get-tuple-element.597, ...), kind=kLoop, calls=%fused_computation.20.clone.1 | loop fusion | flops 27249152 | bytes 8499200 | tf_op jit(solution)/shard_map/while/body/eval_jaxpr/reduce_sum | solution.py:74
  137.0 2.6 multiply_reduce_fusion.8
  139.7 8.7 %multiply_reduce_fusion.9 = (f32[512]{0:T(512)S(1)}, f32[512]{0:T(512)S(1)}, f32[512]{0:T(512)S(1)}, f32[4096]{0:T(1024)S(1)}, f32[4096]{0:T(1024)S(1)}, /*index=5*/f32[4096]{0:T(1024)S(1)}) fusion(f32[512,4096]{1,0:T(8,128)S(1)} %get-tuple-element.596, f32[4096]{0:T(1024)S(1)} %bitcast.171, f32[512]{0:T(512)S(1)} %get-tuple-element.597, ...), kind=kLoop, calls=%fused_computation.20.clone.1 | loop fusion | flops 27249152 | bytes 8499200 | tf_op jit(solution)/shard_map/while/body/eval_jaxpr/reduce_sum | solution.py:74
  148.8 2.6 multiply_reduce_fusion.8
  151.5 8.7 %multiply_reduce_fusion.9 = (f32[512]{0:T(512)S(1)}, f32[512]{0:T(512)S(1)}, f32[512]{0:T(512)S(1)}, f32[4096]{0:T(1024)S(1)}, f32[4096]{0:T(1024)S(1)}, /*index=5*/f32[4096]{0:T(1024)S(1)}) fusion(f32[512,4096]{1,0:T(8,128)S(1)} %get-tuple-element.596, f32[4096]{0:T(1024)S(1)} %bitcast.171, f32[512]{0:T(512)S(1)} %get-tuple-element.597, ...), kind=kLoop, calls=%fused_computation.20.clone.1 | loop fusion | flops 27249152 | bytes 8499200 | tf_op jit(solution)/shard_map/while/body/eval_jaxpr/reduce_sum | solution.py:74
  160.6 2.6 multiply_reduce_fusion.8
  163.3 8.7 %multiply_reduce_fusion.9 = (f32[512]{0:T(512)S(1)}, f32[512]{0:T(512)S(1)}, f32[512]{0:T(512)S(1)}, f32[4096]{0:T(1024)S(1)}, f32[4096]{0:T(1024)S(1)}, /*index=5*/f32[4096]{0:T(1024)S(1)}) fusion(f32[512,4096]{1,0:T(8,128)S(1)} %get-tuple-element.596, f32[4096]{0:T(1024)S(1)} %bitcast.171, f32[512]{0:T(512)S(1)} %get-tuple-element.597, ...), kind=kLoop, calls=%fused_computation.20.clone.1 | loop fusion | flops 27249152 | bytes 8499200 | tf_op jit(solution)/shard_map/while/body/eval_jaxpr/reduce_sum | solution.py:74
  172.4 2.6 multiply_reduce_fusion.8
  175.1 8.7 %multiply_reduce_fusion.9 = (f32[512]{0:T(512)S(1)}, f32[512]{0:T(512)S(1)}, f32[512]{0:T(512)S(1)}, f32[4096]{0:T(1024)S(1)}, f32[4096]{0:T(1024)S(1)}, /*index=5*/f32[4096]{0:T(1024)S(1)}) fusion(f32[512,4096]{1,0:T(8,128)S(1)} %get-tuple-element.596, f32[4096]{0:T(1024)S(1)} %bitcast.171, f32[512]{0:T(512)S(1)} %get-tuple-element.597, ...), kind=kLoop, calls=%fused_computation.20.clone.1 | loop fusion | flops 27249152 | bytes 8499200 | tf_op jit(solution)/shard_map/while/body/eval_jaxpr/reduce_sum | solution.py:74
  184.1 2.6 multiply_reduce_fusion.8
  186.8 8.7 %multiply_reduce_fusion.9 = (f32[512]{0:T(512)S(1)}, f32[512]{0:T(512)S(1)}, f32[512]{0:T(512)S(1)}, f32[4096]{0:T(1024)S(1)}, f32[4096]{0:T(1024)S(1)}, /*index=5*/f32[4096]{0:T(1024)S(1)}) fusion(f32[512,4096]{1,0:T(8,128)S(1)} %get-tuple-element.596, f32[4096]{0:T(1024)S(1)} %bitcast.171, f32[512]{0:T(512)S(1)} %get-tuple-element.597, ...), kind=kLoop, calls=%fused_computation.20.clone.1 | loop fusion | flops 27249152 | bytes 8499200 | tf_op jit(solution)/shard_map/while/body/eval_jaxpr/reduce_sum | solution.py:74
  195.9 2.6 multiply_reduce_fusion.8
  198.6 8.7 %multiply_reduce_fusion.9 = (f32[512]{0:T(512)S(1)}, f32[512]{0:T(512)S(1)}, f32[512]{0:T(512)S(1)}, f32[4096]{0:T(1024)S(1)}, f32[4096]{0:T(1024)S(1)}, /*index=5*/f32[4096]{0:T(1024)S(1)}) fusion(f32[512,4096]{1,0:T(8,128)S(1)} %get-tuple-element.596, f32[4096]{0:T(1024)S(1)} %bitcast.171, f32[512]{0:T(512)S(1)} %get-tuple-element.597, ...), kind=kLoop, calls=%fused_computation.20.clone.1 | loop fusion | flops 27249152 | bytes 8499200 | tf_op jit(solution)/shard_map/while/body/eval_jaxpr/reduce_sum | solution.py:74
  207.7 20.8 %all-gather.4 = f32[16,1,4096]{2,1,0:T(1,128)S(1)} all-gather(f32[1,1,4096]{2,1,0:T(1,128)S(1)} %reshape.122), channel_id=1, replica_groups=mesh['src'=16,'tgt'=16] {'tgt'}, dimensions={0}, use_global_device_ids=true | all-gather | bytes 278528 | tf_op jit(solution)/shard_map/all_gather | solution.py:22
  228.6 17.0 %all-gather.5 = f32[16,1,4096]{2,1,0:T(1,128)S(1)} all-gather(f32[1,1,4096]{2,1,0:T(1,128)S(1)} %reshape.124), channel_id=1, replica_groups=mesh['src'=16,'tgt'=16] {'tgt'}, dimensions={0}, use_global_device_ids=true | all-gather | bytes 278528 | tf_op jit(solution)/shard_map/all_gather | solution.py:22
  245.7 18.5 %all-gather.6 = f32[16,1,4096]{2,1,0:T(1,128)S(1)} all-gather(f32[1,1,4096]{2,1,0:T(1,128)S(1)} %reshape.126), channel_id=1, replica_groups=mesh['src'=16,'tgt'=16] {'tgt'}, dimensions={0}, use_global_device_ids=true | all-gather | bytes 278528 | tf_op jit(solution)/shard_map/all_gather | solution.py:22
  264.2 17.0 %all-gather.7 = f32[16,1,4096]{2,1,0:T(1,128)S(1)} all-gather(f32[1,1,4096]{2,1,0:T(1,128)S(1)} %reshape.128), channel_id=1, replica_groups=mesh['src'=16,'tgt'=16] {'tgt'}, dimensions={0}, use_global_device_ids=true | all-gather | bytes 278528 | tf_op jit(solution)/shard_map/all_gather | solution.py:22
  281.2 38.6 %all-gather = f32[65536]{0:T(1024)S(1)} all-gather(f32[4096]{0:T(1024)S(1)} %get-tuple-element.191), channel_id=2, replica_groups=mesh['src'=16,'tgt'=16] {'src'}, dimensions={0}, use_global_device_ids=true | all-gather | bytes 278528 | tf_op jit(solution)/shard_map/all_gather | solution.py:22
  319.8 40.4 %all-gather.1 = f32[65536]{0:T(1024)S(1)} all-gather(f32[4096]{0:T(1024)S(1)} %get-tuple-element.192), channel_id=3, replica_groups=mesh['src'=16,'tgt'=16] {'src'}, dimensions={0}, use_global_device_ids=true | all-gather | bytes 278528 | tf_op jit(solution)/shard_map/all_gather | solution.py:22
  360.3 37.1 %all-gather.2 = f32[65536]{0:T(1024)S(1)} all-gather(f32[4096]{0:T(1024)S(1)} %get-tuple-element.193), channel_id=4, replica_groups=mesh['src'=16,'tgt'=16] {'src'}, dimensions={0}, use_global_device_ids=true | all-gather | bytes 278528 | tf_op jit(solution)/shard_map/all_gather | solution.py:22
  397.4 40.5 %all-gather.3 = f32[65536]{0:T(1024)S(1)} all-gather(f32[4096]{0:T(1024)S(1)} %get-tuple-element.194), channel_id=5, replica_groups=mesh['src'=16,'tgt'=16] {'src'}, dimensions={0}, use_global_device_ids=true | all-gather | bytes 278528 | tf_op jit(solution)/shard_map/all_gather | solution.py:22
  438.6 2.4 while.57
  441.1 2.4 while.58
  (312 shorter events, 23.8 us)
Async XLA Ops:
  7.2 19.7 %copy-start = (bf16[128,128]{1,0:T(8,128)(2,1)S(1)}, bf16[128,128]{1,0:T(8,128)(2,1)}, u32[]{:S(2)}) copy-start(bf16[128,128]{1,0:T(8,128)(2,1)} %param.13) | copy-start | bytes 98308
  7.2 106.2 %all-gather.10.cloned.1.call-start = ((), (), s32[]{:S(2)}) async-start(), calls=%async_computation.1 | async-start | bytes 1114112 | tf_op jit(solution)/shard_map/all_gather | solution.py:110
  8.1 8.4 %collective-permute-start = (bf16[2,1,256,128]{3,2,1,0:T(8,128)(2,1)S(1)}, bf16[2,1,256,128]{3,2,1,0:T(8,128)(2,1)S(1)}, u32[]{:S(2)}, u32[]{:S(2)}) collective-permute-start(bf16[2,1,256,128]{3,2,1,0:T(8,128)(2,1)S(1)} %pad_maximum_fusion), channel_id=1, source_target_pairs={{0,1},{1,2},{2,3},{3,4},{4,5},{5,6},{6,7},{7,8},{8,9},{9,10},{10,1... | collective-permute-start | bytes 393224 | tf_op jit(solution)/shard_map/ppermute | solution.py:13
  10.0 8.3 %collective-permute-start.1 = (bf16[2,1,256,128]{3,2,1,0:T(8,128)(2,1)S(1)}, bf16[2,1,256,128]{3,2,1,0:T(8,128)(2,1)S(1)}, u32[]{:S(2)}, u32[]{:S(2)}) collective-permute-start(bf16[2,1,256,128]{3,2,1,0:T(8,128)(2,1)S(1)} %pad_maximum_fusion), channel_id=1, source_target_pairs={{1,0},{2,1},{3,2},{4,3},{5,4},{6,5},{7,6},{8,7},{9,8},{10,9},{11,1... | collective-permute-start | bytes 393224 | tf_op jit(solution)/shard_map/ppermute | solution.py:16
  30.0 24.8 %all-to-all-start = ((bf16[16,1,256,128]{3,2,1,0:T(8,128)(2,1)}), bf16[16,1,256,128]{3,2,1,0:T(8,128)(2,1)S(1)}, u32[]{:S(2)}, u32[]{:S(2)}) async-start(bf16[16,1,256,128]{3,2,1,0:T(8,128)(2,1)} %stack.36), calls=%async_computation | async-start | bytes 2097152 | tf_op jit(solution)/shard_map/all_to_all | solution.py:117
Sparse Core Ops, SparseCore 0:
  28.9 84.3 all-gather.9
